TPU v7x, 32 devices: a whole 2x2x4 slice. The times are simulated.
32 devices in a mesh: feat: 8 (over z, core), node: 4 (over y, x).
Axes of the slice: x: 2, y: 2, z: 4, core: 2. Of those that a mesh axis runs over, the one named last changes fastest.
Arguments:
- node_features: bfloat16 [1024, 4, 1024], P('feat', 'node'), may hold values from -6 to 6
- weight: bfloat16 [1024, 256], P('feat'), may hold values from -0.1875 to 0.1875
- out_bias: float32 [256], replicated, may hold values from -3 to 3
- edge_tiles: bfloat16 [4, 8, 8, 128, 128], P('node', 'feat'), may hold values from 0.049804688 to 1
- tile_column: int32 [4, 8, 8], P('node', 'feat'), may hold values from 0 to 7, as said below
- tile_count: int32 [4, 8], P('node', 'feat'), may hold values from 1 to 8, as said below
- grad_hidden: bfloat16 [4, 1024, 256], P('node', 'feat'), may hold values from -6 to 6
Outputs:
- hidden: bfloat16 [4, 1024, 256], P('node', 'feat')
- grad_features: bfloat16 [1024, 4, 1024], P('feat', 'node')
- weight_grad: float32 [1024, 256], P('feat')
Inputs may be any that keep to these rules, and one draw needn't show every extreme that they name: `tile_column`: the 8 column blocks listed for one row block are distinct, live slots or not. `tile_count`: slots of a row block beyond its count are ignored. In every cluster some row block has exactly 8 live tiles.
All inputs are finite; a program needn't handle non-finite values.
Results may differ from a plain program's by a relative error of at most 0.007.
Values may be sent and summed in bfloat16 or wider, within the bound.
A program may use at most 64 MiB of HBM per device.

v0:
```python
import math

import jax
import jax.numpy as jnp
from jax import lax
from jax.sharding import PartitionSpec as P


def gelu_tanh(pre_value):
    return jax.nn.gelu(pre_value, approximate=True)


def body(node_features, weight, out_bias, edge_tiles, tile_column, tile_count, grad_hidden):
    feat_dev, clusters, cluster_rows = node_features.shape
    blocks = lax.axis_size("feat")
    tile_rows = cluster_rows // blocks
    hidden_width = weight.shape[1]
    summed_rows = lax.psum_scatter(
        jnp.einsum("fqr,fh->rqh", node_features, weight, preferred_element_type=jnp.float32),
        "feat",
        scatter_dimension=0,
        tiled=True,
    )
    own_proj = jnp.transpose(summed_rows, (1, 0, 2))
    own_rounded = own_proj.astype(jnp.bfloat16)
    all_proj = lax.all_gather(own_rounded, "feat", axis=1, tiled=True)
    blocks_proj = all_proj.reshape(clusters, blocks, tile_rows, hidden_width)
    my_tiles = edge_tiles[:, 0]
    my_cols = tile_column[:, 0]
    counts = tile_count[:, 0]
    slot_ids = jnp.arange(my_tiles.shape[1], dtype=jnp.int32)
    live_mask = (slot_ids[None, :] < counts[:, None]).astype(jnp.bfloat16)
    masked = my_tiles * live_mask[:, :, None, None]
    degree = jnp.sum(masked, axis=(1, 3), dtype=jnp.float32)
    cluster_ids = jnp.arange(clusters, dtype=jnp.int32)[:, None]
    chosen = blocks_proj[cluster_ids, my_cols]
    summed = jnp.einsum("qsij,qsjh->qih", masked, chosen, preferred_element_type=jnp.float32)
    row_scale = lax.rsqrt(degree)[:, :, None]
    pre_act = summed * row_scale + out_bias
    activated, backward = jax.vjp(gelu_tanh, pre_act)
    hidden = activated.astype(jnp.bfloat16)
    (grad_pre,) = backward(grad_hidden.astype(jnp.float32))
    scaled = (grad_pre * row_scale).astype(jnp.bfloat16)
    tile_terms = jnp.einsum(
        "qsij,qih->qsjh", masked, scaled, preferred_element_type=jnp.float32
    ).astype(jnp.bfloat16)
    outgoing = (
        jnp.zeros((blocks, clusters, tile_rows, hidden_width), jnp.bfloat16)
        .at[my_cols, cluster_ids]
        .set(tile_terms)
    )
    arrived = lax.all_to_all(outgoing, "feat", split_axis=0, concat_axis=0, tiled=True)
    own_grad = jnp.sum(arrived, axis=0, dtype=jnp.float32).astype(jnp.bfloat16)
    all_grad = lax.all_gather(own_grad, "feat", axis=1, tiled=True)
    grad_features = jnp.einsum(
        "fh,qrh->fqr", weight, all_grad, preferred_element_type=jnp.float32
    ).astype(jnp.bfloat16)
    partial_grad = jnp.einsum(
        "fqr,qrh->fh", node_features, all_grad, preferred_element_type=jnp.float32
    )
    total_nodes = clusters * lax.axis_size("node") * cluster_rows
    weight_grad = lax.psum(partial_grad, "node") * (1.0 / math.sqrt(total_nodes))
    return (hidden, grad_features, weight_grad)


def solution(mesh):
    return jax.shard_map(
        body,
        mesh=mesh,
        in_specs=(
            P("feat", "node", None),
            P("feat", None),
            P(),
            P("node", "feat", None, None, None),
            P("node", "feat", None),
            P("node", "feat"),
            P("node", "feat", None),
        ),
        out_specs=(P("node", "feat", None), P("feat", "node", None), P("feat", None)),
        check_vma=False,
    )
```

profile of v0, /device:TPU:0, one launch (start us, length us, event | category | flops | bytes accessed | tf_op | source)
XLA Modules:
  0.0 150.2 jit_solution(10850708865901555610)
XLA Ops:
  7.2 0.0 reduce-scatter.2.cloned.1.call-start
  7.2 0.9 copy-done
  8.1 2.1 %convolution_bitcast_fusion = f32[1024,1,256]{0,2,1:T(8,128)} fusion(bf16[128,256]{1,0:T(8,128)(2,1)} %param.8, bf16[128,1,1024]{2,0,1:T(8,128)(2,1)S(1)} %copy-done), kind=kOutput, calls=%fused_computation.2 | convolution fusion | flops 67108864 | bytes 1376256 | tf_op jit(solution)/shard_map/fqr,fh->rqh/dot_general | solution.py:19
  10.3 0.0 reduce-scatter.2.cloned.1.call-update
  11.0 0.2 copy-done.1
  11.2 0.2 convert_reduce_fusion
  11.4 0.6 copy-done.5
  12.1 33.3 %reduce-scatter.2.cloned.1.call-done = f32[128,1,256]{0,2,1:T(8,128)} async-done(((f32[1024,1,256]{0,2,1:T(8,128)}), f32[128,1,256]{0,2,1:T(8,128)}) %reduce-scatter.2.cloned.1.call-update) | async-done | bytes 131088 | tf_op jit(solution)/shard_map/reduce_scatter | solution.py:18
  45.5 0.9 convert_element_type.64
  46.4 14.0 %all-gather = bf16[1024,1,256]{0,2,1:T(8,128)(2,1)S(1)} all-gather(bf16[128,1,256]{0,2,1:T(8,128)(2,1)S(1)} %convert_element_type.64), channel_id=2, replica_groups=mesh['feat'=8,'node'=4] {'feat'}, dimensions={0}, use_global_device_ids=true | all-gather | bytes 589824 | tf_op jit(solution)/shard_map/all_gather | solution.py:26
  60.4 0.2 copy.22
  60.6 0.6 gather_fusion
  61.2 0.1 copy-done.3
  61.3 0.3 fusion.2
  61.5 0.6 copy-done.4
  62.1 0.4 convolution_convert_fusion
  62.5 0.8 broadcast.100
  63.4 2.5 %scatter_fusion = bf16[8,128,256]{2,1,0:T(8,128)(2,1)} fusion(bf16[8,128,256]{2,1,0:T(8,128)(2,1)} %broadcast.100, s32[8]{0:T(128)S(1)} %fusion.32, bf16[8,128,256]{2,1,0:T(8,128)(2,1)S(1)} %convolution_convert_fusion), kind=kCustom, calls=%fused_computation.1 | custom fusion | bytes 1572896 | tf_op jit(solution)/shard_map/scatter | solution.py:50
  65.8 3.5 %all-to-all-start = ((bf16[8,1,128,256]{3,2,1,0:T(8,128)(2,1)}), bf16[8,1,128,256]{3,2,1,0:T(8,128)(2,1)S(1)}, u32[]{:S(2)}, u32[]{:S(2)}) async-start(bf16[8,1,128,256]{3,2,1,0:T(8,128)(2,1)} %bitcast.21), calls=%async_computation.1 | async-start | bytes 1048576 | tf_op jit(solution)/shard_map/all_to_all | solution.py:52
  69.3 0.0 all-reduce.4.cloned.1.call-start
  69.4 0.7 fusion.31
  70.0 14.6 %all-to-all-done = bf16[8,1,128,256]{3,2,1,0:T(8,128)(2,1)S(1)} async-done(((bf16[8,1,128,256]{3,2,1,0:T(8,128)(2,1)}), bf16[8,1,128,256]{3,2,1,0:T(8,128)(2,1)S(1)}, u32[]{:S(2)}, u32[]{:S(2)}) %all-to-all-start) | async-done | bytes 524320 | tf_op jit(solution)/shard_map/all_to_all | solution.py:52
  84.6 0.1 reduce_sum.24
  84.7 14.9 %all-gather.1 = bf16[1024,256]{1,0:T(8,128)(2,1)S(1)} all-gather(bf16[128,256]{1,0:T(8,128)(2,1)S(1)} %reduce_sum.24), channel_id=3, replica_groups=mesh['feat'=8,'node'=4] {'feat'}, dimensions={0}, use_global_device_ids=true | all-gather | bytes 589824 | tf_op jit(solution)/shard_map/all_gather | solution.py:54
  99.6 1.0 convolution_bitcast_fusion.1
  100.6 0.0 all-reduce.4.cloned.1.call-update
  100.6 0.8 copy-done.2
  101.5 0.3 fusion
  101.8 0.9 copy.19
  102.6 39.1 %all-reduce.4.cloned.1.call-done = f32[128,256]{0,1:T(8,128)} async-done(((f32[128,256]{0,1:T(8,128)}), f32[128,256]{0,1:T(8,128)}) %all-reduce.4.cloned.1.call-update) | async-done | bytes 131088 | tf_op jit(solution)/shard_map/psum | solution.py:62
  141.7 0.9 broadcast_multiply_fusion
  142.6 0.8 copy.20
  (12 shorter events, 0.1 us)
Async XLA Ops:
  7.2 1.0 copy-start
  7.2 38.3 %reduce-scatter.2.cloned.1.call-start = ((), (), s32[]{:S(2)}) async-start(), calls=%async_computation.2 | async-start | bytes 1179648 | tf_op jit(solution)/shard_map/reduce_scatter | solution.py:18
  10.3 1.0 copy-start.1
  11.4 0.7 copy-start.5
  60.6 0.7 copy-start.3
  61.3 0.8 copy-start.4
  65.8 18.8 %all-to-all-start = ((bf16[8,1,128,256]{3,2,1,0:T(8,128)(2,1)}), bf16[8,1,128,256]{3,2,1,0:T(8,128)(2,1)S(1)}, u32[]{:S(2)}, u32[]{:S(2)}) async-start(bf16[8,1,128,256]{3,2,1,0:T(8,128)(2,1)} %bitcast.21), calls=%async_computation.1 | async-start | bytes 1048576 | tf_op jit(solution)/shard_map/all_to_all | solution.py:52
  69.3 72.3 %all-reduce.4.cloned.1.call-start = ((), (), s32[]{:S(2)}) async-start(), calls=%async_computation.3 | async-start | bytes 262144 | tf_op jit(solution)/shard_map/psum | solution.py:62
  100.6 0.8 copy-start.2
Sparse Core Ops, SparseCore 0:
  10.4 35.0 reduce-scatter.1
  100.8 40.8 all-reduce.3
where the time goes:
time: 151 us; the launch traced here: 150 us
  waiting for transfers between devices  87 us (58%)
  blocking collectives  28.9 us (19%)
  between operations  14.8 us (10%)
  local copies, waits for them, and re-layouts  8.93 us (6%)
  matrix products  4.12 us (3%)
  starting transfers between devices  3.57 us (2%)
  other arithmetic  2.8 us (2%)
    psum x1, waiting for transfers between devices, body(): lax.psum(partial_grad, 'node') * (1.0 / math.sqrt(total_nodes))  39.1 us
    reduce_scatter x1, waiting for transfers between devices, body(): lax.psum_scatter(jnp.einsum('fqr,fh->rqh', node_features, weight, preferr...  33.3 us
    all_gather x1, blocking collectives, body(): all_grad = lax.all_gather(own_grad, 'feat', axis=1, tiled=True)  14.9 us
    all_to_all x1, waiting for transfers between devices, body(): lax.all_to_all(outgoing, 'feat', split_axis=0, concat_axis=0, tiled=True)  14.6 us
    all_gather x1, blocking collectives, body(): all_proj = lax.all_gather(own_rounded, 'feat', axis=1, tiled=True)  14 us
    unnamed x14, local copies, waits for them, and re-layouts  4.86 us
    all_to_all x1, starting transfers between devices, body(): lax.all_to_all(outgoing, 'feat', split_axis=0, concat_axis=0, tiled=True)  3.49 us
  transfers between devices with their start and end apart: 3, of which 3 were waited for; matrix products, arithmetic and copies ran while one was open for 1% of the time, Pallas kernels for 0%

commit v1 on v0

v1 whole, which is shorter than its diff:
```python
import functools
import math

import jax
import jax.numpy as jnp
from jax import lax
from jax.experimental import pallas as pl
from jax.experimental.pallas import tpu as pltpu
from jax.sharding import PartitionSpec as P

MESH = pl.DeviceIdType.MESH
F32 = jnp.float32
BF16 = jnp.bfloat16
CHUNKS = 2
ROOT = math.sqrt(2.0 / math.pi)


def flip(index, bit):
    return index + bit * (1 - 2 * ((index // bit) % 2))


def flip_many(index, mask, steps):
    for j in range(steps):
        if (mask >> j) & 1:
            index = flip(index, 1 << j)
    return index


def tn(a, b):
    return lax.dot_general(a, b, (((0,), (0,)), ((), ())), preferred_element_type=F32)


def nt(a, b):
    return lax.dot_general(a, b, (((1,), (1,)), ((), ())), preferred_element_type=F32)


def nn(a, b):
    return lax.dot_general(a, b, (((1,), (0,)), ((), ())), preferred_element_type=F32)


def kernel(sizes, cols, count, feats, weight, bias, tiles, grad_hidden,
           hidden, grad_feat, weight_grad,
           x_send, x_pair, w_pair, a_send, a_pair,
           rs_out, rs_in, gath, part_out, part_in, sc_pair, rt_out, rt_in, ggath, gfwd,
           wg_out, wg_in,
           ex_s, ex_r, rs_s, rs_r, ag_s, ag_r, p_s, p_r, s_s, s_r, rt_s, rt_r,
           gg_s, gg_r, fw_s, fw_r, wg_s, wg_r):
    zs, nodes, slots, tr, fd, hw, total = sizes
    zbits, nbits = zs.bit_length() - 1, nodes.bit_length() - 1
    hc = hw // CHUNKS
    feat_at = lax.axis_index("feat")
    node_at = lax.axis_index("node")
    core = feat_at % 2
    z = feat_at // 2
    mate = {"feat": z * 2 + 1 - core}

    def z_peer(j):
        return {"feat": flip(z, 1 << j) * 2 + core}

    def n_peer(j):
        return {"node": flip(node_at, 1 << j)}

    def push(src, dst, ss, rr, dev):
        copy = pltpu.make_async_remote_copy(
            src_ref=src, dst_ref=dst, send_sem=ss, recv_sem=rr,
            device_id=dev, device_id_type=MESH)
        copy.start()
        sent.append(copy)
        return copy

    sent = []
    barrier = pltpu.get_barrier_semaphore()
    peers = [mate] + [z_peer(j) for j in range(zbits)] + [n_peer(j) for j in range(nbits)]
    for dev in peers:
        pl.semaphore_signal(barrier, inc=1, device_id=dev, device_id_type=MESH)

    zrel = [flip_many(z, r, zbits) for r in range(zs)]

    def rows_of(r, parity):
        return pl.multiple_of((zrel[r] * 2 + parity) * tr, tr)

    for r in range(zs):
        x_pair[r, 0:fd, :] = feats[:, pl.ds(rows_of(r, core), tr)]
        x_send[r] = feats[:, pl.ds(rows_of(r, 1 - core), tr)]
    w_pair[0:fd, :] = weight[...]
    pl.semaphore_wait(barrier, len(peers))
    ex_x = push(x_send, x_pair.at[:, pl.ds(fd, fd), :], ex_s.at[0], ex_r.at[0], mate)
    ex_w = push(weight, w_pair.at[pl.ds(fd, fd)], ex_s.at[1], ex_r.at[1], mate)

    degree = jnp.zeros((tr, 1), F32)
    live = count[0]

    def listed(block):
        where = jnp.int32(0)
        alive = jnp.int32(0)
        for s in range(slots):
            hit = cols[s] == block
            where = jnp.where(hit, s, where)
            alive = jnp.where(hit, jnp.where(s < live, 1, 0), alive)
        return tiles[where].astype(F32) * alive.astype(F32)

    for r in range(zs):
        other = listed(zrel[r] * 2 + 1 - core)
        a_send[:, r * tr:(r + 1) * tr] = other.astype(BF16)
        mine = listed(zrel[r] * 2 + core)
        a_pair[0:tr, r * tr:(r + 1) * tr] = mine.astype(BF16)
        degree = degree + jnp.sum(mine + other, axis=1, keepdims=True)
    ex_a = push(a_send, a_pair.at[pl.ds(tr, tr)], ex_s.at[2], ex_r.at[2], mate)
    row_scale = lax.rsqrt(degree)
    ex_x.wait_recv()
    ex_w.wait_recv()

    def hs(k):
        return slice(k * hc, (k + 1) * hc)

    def slot_of(j):
        return sum(zs >> (i + 1) for i in range(j))

    def rs_first(k, make, out, into, ss, rr):
        kept = {}
        n = zs // 2
        for m in range(n):
            out[k, m] = make(1 + 2 * m).astype(BF16)
        copies = [push(out.at[k, pl.ds(0, n)], into.at[k, pl.ds(0, n)],
                       ss.at[k, 0], rr.at[k, 0], z_peer(0))]
        for m in range(n):
            kept[2 * m] = make(2 * m)
        return kept, copies[0]

    def rs_next(k, j, kept, copy, out, into, ss, rr):
        base = slot_of(j - 1)
        copy.wait_recv()
        step = 1 << j
        held = {}
        for m in range(zs >> j):
            held[m * step] = kept[m * step] + into[k, base + m].astype(F32)
        if j == zbits:
            return held[0]
        n = zs >> (j + 1)
        at = slot_of(j)
        for m in range(n):
            out[k, at + m] = held[step + 2 * step * m].astype(BF16)
        nxt = push(out.at[k, pl.ds(at, n)], into.at[k, pl.ds(at, n)],
                   ss.at[k, j], rr.at[k, j], z_peer(j))
        return {2 * step * m: held[2 * step * m] for m in range(n)}, nxt

    def gather_send(k, r, low, buf, ss, rr, waits):
        for j in reversed(range(low)):
            slot = r + (1 << j)
            waits[slot] = push(buf.at[k, r], buf.at[k, slot], ss.at[k, slot],
                               rr.at[k, slot], z_peer(j))

    ks = range(CHUNKS)

    def reduce_scatter(make, out, into, ss, rr):
        state = [rs_first(k, functools.partial(make, k), out, into, ss, rr) for k in ks]
        for j in range(1, zbits):
            state = [rs_next(k, j, *state[k], out, into, ss, rr) for k in ks]
        return state

    def gather(k_waits, k, j, buf, ss, rr, seen):
        step = 1 << (j + 1)
        for m in range(zs // step):
            slot = m * step + (1 << j)
            k_waits[slot].wait_recv()
            gather_send(k, slot, j, buf, ss, rr, k_waits)
            seen(k, slot)

    def project(k, r):
        return tn(x_pair[r], w_pair[:, hs(k)])

    state = reduce_scatter(project, rs_out, rs_in, rs_s, rs_r)
    waits = [dict() for _ in ks]
    for k in ks:
        own = rs_next(k, zbits, *state[k], rs_out, rs_in, rs_s, rs_r)
        gath[k, 0] = own.astype(BF16)
        gather_send(k, 0, zbits, gath, ag_s, ag_r, waits[k])
    for j in reversed(range(1, zbits)):
        for k in ks:
            gather(waits[k], k, j, gath, ag_s, ag_r, lambda k, r: None)
    ex_a.wait_recv()
    mine_sum, parts = [], []
    for k in ks:
        gather(waits[k], k, 0, gath, ag_s, ag_r, lambda k, r: None)
        both = nn(a_pair[...], gath[k].reshape(zs * tr, hc))
        part_out[k] = both[tr:]
        parts.append(push(part_out.at[k], part_in.at[k], p_s.at[k], p_r.at[k], mate))
        mine_sum.append(both[:tr])
    scs = []
    for k in ks:
        parts[k].wait_recv()
        v = (mine_sum[k] + part_in[k]) * row_scale + bias[:, hs(k)]
        v2 = v * v
        t = jnp.tanh(ROOT * (v + 0.044715 * v2 * v))
        hidden[:, hs(k)] = (0.5 * v * (1.0 + t)).astype(BF16)
        slope = 0.5 * (1.0 + t) + 0.5 * v * (1.0 - t * t) * (ROOT * (1.0 + 3 * 0.044715 * v2))
        grad_pre = grad_hidden[:, hs(k)].astype(F32) * slope
        sc_pair[k, 0:tr] = (grad_pre * row_scale).astype(BF16)
        scs.append(push(sc_pair.at[k, pl.ds(0, tr)], sc_pair.at[k, pl.ds(tr, tr)],
                        s_s.at[k], s_r.at[k], mate))

    def terms(k, r):
        if r == 1:
            scs[k].wait_recv()
        return tn(a_pair[:, r * tr:(r + 1) * tr], sc_pair[k])

    state = reduce_scatter(terms, rt_out, rt_in, rt_s, rt_r)
    waits = [dict() for _ in ks]
    fwd = [dict() for _ in ks]

    def forward(k, r):
        fwd[k][r] = push(ggath.at[k, r], gfwd.at[k, r], fw_s.at[k, r], fw_r.at[k, r], mate)

    for k in ks:
        own = rs_next(k, zbits, *state[k], rt_out, rt_in, rt_s, rt_r)
        ggath[k, 0] = own.astype(BF16)
        gather_send(k, 0, zbits, ggath, gg_s, gg_r, waits[k])
        forward(k, 0)
    for j in reversed(range(1, zbits)):
        for k in ks:
            gather(waits[k], k, j, ggath, gg_s, gg_r, forward)
    node_state = []
    scale = 1.0 / math.sqrt(total)

    def node_send(k, i, value):
        j = (i + k) % nbits
        wg_out[k, i] = value.astype(BF16)
        return push(wg_out.at[k, i], wg_in.at[k, i], wg_s.at[k, i], wg_r.at[k, i], n_peer(j))

    for k in ks:
        gather(waits[k], k, 0, ggath, gg_s, gg_r, forward)
        acc = jnp.zeros((fd, hc), F32)
        for r in range(zs):
            acc = acc + nn(x_pair[r, 0:fd, :], ggath[k, r])
        for r in range(zs):
            fwd[k][r].wait_recv()
            acc = acc + nn(x_send[r], gfwd[k, r])
        node_state.append(node_send(k, 0, acc))
    for r in range(zs):
        for parity, buf in ((core, ggath), (1 - core, gfwd)):
            total_rows = nt(weight[:, hs(0)], buf[0, r])
            for k in range(1, CHUNKS):
                total_rows = total_rows + nt(weight[:, hs(k)], buf[k, r])
            grad_feat[:, pl.ds(rows_of(r, parity), tr)] = total_rows.astype(BF16)
    for i in range(1, nbits + 1):
        for k in ks:
            node_state[k].wait_recv()
            value = wg_out[k, i - 1].astype(F32) + wg_in[k, i - 1].astype(F32)
            if i < nbits:
                node_state[k] = node_send(k, i, value)
            else:
                weight_grad[:, hs(k)] = value * scale
    for copy in sent:
        copy.wait_send()


def body(node_features, weight, out_bias, edge_tiles, tile_column, tile_count, grad_hidden):
    fd, _, rows = node_features.shape
    blocks = lax.axis_size("feat")
    nodes = lax.axis_size("node")
    zs = blocks // 2
    nbits = nodes.bit_length() - 1
    tr = rows // blocks
    hw = weight.shape[1]
    hc = hw // CHUNKS
    slots = edge_tiles.shape[2]
    sizes = (zs, nodes, slots, tr, fd, hw, nodes * rows)
    vmem = pl.BlockSpec(memory_space=pltpu.VMEM)
    smem = pl.BlockSpec(memory_space=pltpu.SMEM)
    dma = pltpu.SemaphoreType.DMA
    c = CHUNKS
    scratch = [
        pltpu.VMEM((zs, fd, tr), BF16),
        pltpu.VMEM((zs, 2 * fd, tr), BF16),
        pltpu.VMEM((2 * fd, hw), BF16),
        pltpu.VMEM((tr, zs * tr), BF16),
        pltpu.VMEM((2 * tr, zs * tr), BF16),
        pltpu.VMEM((c, zs, tr, hc), BF16),
        pltpu.VMEM((c, zs, tr, hc), BF16),
        pltpu.VMEM((c, zs, tr, hc), BF16),
        pltpu.VMEM((c, tr, hc), F32),
        pltpu.VMEM((c, tr, hc), F32),
        pltpu.VMEM((c, 2 * tr, hc), BF16),
        pltpu.VMEM((c, zs, tr, hc), BF16),
        pltpu.VMEM((c, zs, tr, hc), BF16),
        pltpu.VMEM((c, zs, tr, hc), BF16),
        pltpu.VMEM((c, zs, tr, hc), BF16),
        pltpu.VMEM((c, nbits, fd, hc), BF16),
        pltpu.VMEM((c, nbits, fd, hc), BF16),
    ]
    for shape in ((3,), (c, zs), (c, zs), (c,), (c,), (c, zs), (c, zs), (c, zs), (c, nbits)):
        scratch += [dma(shape), dma(shape)]
    hidden, grad_feat, weight_grad = pl.pallas_call(
        functools.partial(kernel, sizes),
        out_shape=(
            jax.ShapeDtypeStruct((tr, hw), BF16),
            jax.ShapeDtypeStruct((fd, rows), BF16),
            jax.ShapeDtypeStruct((fd, hw), F32),
        ),
        in_specs=[smem, smem, vmem, vmem, vmem, vmem, vmem],
        out_specs=(vmem, vmem, vmem),
        scratch_shapes=scratch,
        compiler_params=pltpu.CompilerParams(
            collective_id=0, has_side_effects=True, vmem_limit_bytes=48 * 1024 * 1024
        ),
        name="sage",
    )(
        tile_column.reshape(slots),
        tile_count.reshape(1),
        node_features.reshape(fd, rows),
        weight,
        out_bias.reshape(1, hw),
        edge_tiles.reshape(slots, tr, tr),
        grad_hidden.reshape(tr, hw),
    )
    return (hidden[None], grad_feat[:, None, :], weight_grad)


def solution(mesh):
    return jax.shard_map(
        body,
        mesh=mesh,
        in_specs=(
            P("feat", "node", None),
            P("feat", None),
            P(),
            P("node", "feat", None, None, None),
            P("node", "feat", None),
            P("node", "feat"),
            P("node", "feat", None),
        ),
        out_specs=(P("node", "feat", None), P("feat", "node", None), P("feat", None)),
        check_vma=False,
    )
```

time: 151 us -> 54.7 us (0.36)
  waiting for transfers between devices: 87 us -> 0 us
  Pallas kernels: 0 us -> 46.8 us
  blocking collectives: 28.9 us -> 0 us
  between operations: 14.8 us -> 1.31 us
  matrix products: 4.12 us -> 0 us
  starting transfers between devices: 3.57 us -> 0 us
  other arithmetic: 2.8 us -> 0 us
  local copies, waits for them, and re-layouts: 8.93 us -> 6.23 us
    pallas_call x0 -> x1, Pallas kernels: none -> 46.8 us  [body(): pl.pallas_call(functools.partial(kernel, sizes), out_shape=(jax.ShapeDtyp...]
    psum x1 -> x0, waiting for transfers between devices: 39.1 us -> none  [body(): lax.psum(partial_grad, 'node') * (1.0 / math.sqrt(total_nodes))]
    reduce_scatter x1 -> x0, waiting for transfers between devices: 33.3 us -> none  [body(): lax.psum_scatter(jnp.einsum('fqr,fh->rqh', node_features, weight, preferr...]
    all_gather x2 -> x0, blocking collectives: 28.9 us -> none  [the longest x1 14.9 us: body(): all_grad = lax.all_gather(own_grad, 'feat', axis=1, tiled=True)]
    all_to_all x1 -> x0, waiting for transfers between devices: 14.6 us -> none  [body(): lax.all_to_all(outgoing, 'feat', split_axis=0, concat_axis=0, tiled=True)]
    dot_general x5 -> x0, matrix products: 4.12 us -> none  [the longest x1 2.13 us: body(): jnp.einsum('fqr,fh->rqh', node_features, weight, preferred_element_type=j...]
    all_to_all x1 -> x0, starting transfers between devices: 3.49 us -> none  [body(): lax.all_to_all(outgoing, 'feat', split_axis=0, concat_axis=0, tiled=True)]
    scatter x1 -> x0, local copies, waits for them, and re-layouts: 2.46 us -> none  [body(): outgoing = jnp.zeros((blocks, clusters, tile_rows, hidden_width), jnp.bfl...]
  transfers between devices with their start and end apart: 3 -> 0, of which waited for: 3 -> 0; matrix products, arithmetic and copies ran while one was open for 1% -> 0% of each run, Pallas kernels for 0% -> 0%
where the time goes in v1:
time: 54.7 us; the launch traced here: 54.4 us
  Pallas kernels  46.8 us (86%)
  local copies, waits for them, and re-layouts  6.23 us (11%)
  between operations  1.31 us (2%)
    pallas_call x1, Pallas kernels, body(): pl.pallas_call(functools.partial(kernel, sizes), out_shape=(jax.ShapeDtyp...  46.8 us
    unnamed x15, local copies, waits for them, and re-layouts  6.23 us

profile of v1, /device:TPU:0, one launch (start us, length us, event | category | flops | bytes accessed | tf_op | source)
XLA Modules:
  0.0 54.4 jit_solution(17172757699619908297)
XLA Ops:
  1.3 0.0 copy-start.4
  1.3 0.0 copy-start.5
  1.3 0.7 %copy-done.4 = f32[256]{0:T(256)S(1)} copy-done((f32[256]{0:T(256)S(1)}, f32[256]{0:T(256)}, u32[]{:S(2)}) %copy-start.4) | copy-done | bytes 1048
  2.0 0.0 copy-done.5
  2.0 0.0 copy-start
  2.0 0.9 %copy-done = bf16[128,1,1024]{2,0,1:T(8,128)(2,1)S(1)} copy-done((bf16[128,1,1024]{2,0,1:T(8,128)(2,1)S(1)}, bf16[128,1,1024]{2,0,1:T(8,128)(2,1)}, u32[]{:S(2)}) %copy-start) | copy-done | bytes 262168
  2.9 0.0 copy-start.1
  2.9 0.9 %copy-done.1 = bf16[1,1,8,128,128]{4,3,2,1,0:T(8,128)(2,1)S(1)} copy-done((bf16[1,1,8,128,128]{4,3,2,1,0:T(8,128)(2,1)S(1)}, bf16[1,1,8,128,128]{4,3,2,1,0:T(8,128)(2,1)}, u32[]{:S(2)}) %copy-start.1) | copy-done | bytes 262168
  3.9 0.0 copy-start.2
  3.9 0.8 %copy-done.2 = bf16[128,256]{1,0:T(8,128)(2,1)S(1)} copy-done((bf16[128,256]{1,0:T(8,128)(2,1)S(1)}, bf16[128,256]{1,0:T(8,128)(2,1)}, u32[]{:S(2)}) %copy-start.2) | copy-done | bytes 65560
  4.7 0.0 copy-start.3
  4.7 0.8 %copy-done.3 = bf16[1,128,256]{2,1,0:T(8,128)(2,1)S(1)} copy-done((bf16[1,128,256]{2,1,0:T(8,128)(2,1)S(1)}, bf16[1,128,256]{2,1,0:T(8,128)(2,1)}, u32[]{:S(2)}) %copy-start.3) | copy-done | bytes 65560
  5.5 46.8 %sage.1 = (bf16[128,256]{1,0:T(8,128)(2,1)S(1)}, bf16[128,1024]{1,0:T(8,128)(2,1)S(1)}, f32[128,256]{1,0:T(8,128)S(1)}) custom-call(s32[8]{0:T(128)S(1)} %bitcast.15, s32[1]{0:T(128)} %bitcast.8.count, bf16[128,1024]{1,0:T(8,128)(2,1)S(1)} %bitcast.9, bf16[128,256]{1,0:T(8,128)(2,1)S(1)} %copy-done.2, f32[1,256]{1,0:T(1,128)S(1)} %bitcast.14, ...), custom_call_target="tpu_custom_call" | custom-call | tf_op jit(solution)/shard_map/sage/pallas_call | solution.py:293
  52.4 0.6 %copy.14 = bf16[1,128,256]{2,1,0:T(8,128)(2,1)} copy(bf16[1,128,256]{2,1,0:T(8,128)(2,1)S(1)} %bitcast.13) | data formatting | bytes 131072
  53.0 0.7 %copy.15 = bf16[128,1,1024]{2,0,1:T(8,128)(2,1)} copy(bf16[128,1,1024]{2,0,1:T(8,128)(2,1)S(1)} %bitcast.11) | data formatting | bytes 524288
  53.7 0.7 %copy.16 = f32[128,256]{1,0:T(8,128)} copy(f32[128,256]{1,0:T(8,128)S(1)} %get-tuple-element.14) | data formatting | bytes 262144
Async XLA Ops:
  1.3 0.7 %copy-start.4 = (f32[256]{0:T(256)S(1)}, f32[256]{0:T(256)}, u32[]{:S(2)}) copy-start(f32[256]{0:T(256)} %param.9) | copy-start | bytes 3076
  1.3 0.7 %copy-start.5 = (s32[1,1,8]{2,1,0:T(1,128)S(1)}, s32[1,1,8]{2,1,0:T(1,128)}, u32[]{:S(2)}) copy-start(s32[1,1,8]{2,1,0:T(1,128)} %param.11) | copy-start | bytes 100
  2.0 1.0 %copy-start = (bf16[128,1,1024]{2,0,1:T(8,128)(2,1)S(1)}, bf16[128,1,1024]{2,0,1:T(8,128)(2,1)}, u32[]{:S(2)}) copy-start(bf16[128,1,1024]{2,0,1:T(8,128)(2,1)} %param.7) | copy-start | bytes 786436
  2.9 0.9 %copy-start.1 = (bf16[1,1,8,128,128]{4,3,2,1,0:T(8,128)(2,1)S(1)}, bf16[1,1,8,128,128]{4,3,2,1,0:T(8,128)(2,1)}, u32[]{:S(2)}) copy-start(bf16[1,1,8,128,128]{4,3,2,1,0:T(8,128)(2,1)} %param.10) | copy-start | bytes 786436
  3.9 0.8 %copy-start.2 = (bf16[128,256]{1,0:T(8,128)(2,1)S(1)}, bf16[128,256]{1,0:T(8,128)(2,1)}, u32[]{:S(2)}) copy-start(bf16[128,256]{1,0:T(8,128)(2,1)} %weight.1) | copy-start | bytes 196612
  4.7 0.8 %copy-start.3 = (bf16[1,128,256]{2,1,0:T(8,128)(2,1)S(1)}, bf16[1,128,256]{2,1,0:T(8,128)(2,1)}, u32[]{:S(2)}) copy-start(bf16[1,128,256]{2,1,0:T(8,128)(2,1)} %param.13) | copy-start | bytes 196612

commit v2 on v1

v2 whole, which is shorter than its diff:
```python
import functools
import math

import jax
import jax.numpy as jnp
from jax import lax
from jax.experimental import pallas as pl
from jax.experimental.pallas import tpu as pltpu
from jax.sharding import PartitionSpec as P

MESH = pl.DeviceIdType.MESH
F32 = jnp.float32
BF16 = jnp.bfloat16
CHUNKS = 2
ROOT = math.sqrt(2.0 / math.pi)


def flip(index, bit):
    return index + bit * (1 - 2 * ((index // bit) % 2))


def flip_many(index, mask, steps):
    for j in range(steps):
        if (mask >> j) & 1:
            index = flip(index, 1 << j)
    return index


def tn(a, b):
    return lax.dot_general(a, b, (((0,), (0,)), ((), ())), preferred_element_type=F32)


def nt(a, b):
    return lax.dot_general(a, b, (((1,), (1,)), ((), ())), preferred_element_type=F32)


def nn(a, b):
    return lax.dot_general(a, b, (((1,), (0,)), ((), ())), preferred_element_type=F32)


def kernel(sizes, cols_hbm, count_hbm, feats, weight_hbm, bias_hbm, tiles_hbm, grad_hbm,
           hidden, grad_feat, weight_grad,
           cols, count, weight, bias, tiles, grad_hidden, in_s, xa_s, xb_s, xs_s, xs_r,
           x_send, x_pair, w_pair, a_send, a_pair,
           rs_out, rs_in, gath, part_out, part_in, sc_pair, rt_out, rt_in, ggath, gfwd,
           wg_in,
           ex_s, ex_r, rs_s, rs_r, ag_s, ag_r, p_s, p_r, s_s, s_r, rt_s, rt_r,
           gg_s, gg_r, fw_s, fw_r, wg_s, wg_r):
    zs, nodes, slots, tr, fd, hw, total = sizes
    zbits, nbits = zs.bit_length() - 1, nodes.bit_length() - 1
    hc = hw // CHUNKS
    feat_at = lax.axis_index("feat")
    node_at = lax.axis_index("node")
    core = feat_at % 2
    z = feat_at // 2
    mate = {"feat": z * 2 + 1 - core}

    zrel = [flip_many(z, r, zbits) for r in range(zs)]

    def z_peer(r):
        return {"feat": zrel[r] * 2 + core}

    def n_peer(n):
        return {"node": flip_many(node_at, n, nbits)}

    def push(src, dst, ss, rr, dev):
        copy = pltpu.make_async_remote_copy(
            src_ref=src, dst_ref=dst, send_sem=ss, recv_sem=rr,
            device_id=dev, device_id_type=MESH)
        copy.start()
        sent.append(copy)
        return copy

    sent = []
    far = list(reversed(range(1, zs)))
    barrier = pltpu.get_barrier_semaphore()
    peers = [mate] + [z_peer(r) for r in range(1, zs)] + [n_peer(n) for n in range(1, nodes)]
    for dev in peers:
        pl.semaphore_signal(barrier, inc=1, device_id=dev, device_id_type=MESH)

    def rows_of(r, parity):
        return pl.multiple_of((zrel[r] * 2 + parity) * tr, tr)

    def fetch(src, dst, sem):
        copy = pltpu.make_async_copy(src, dst, sem)
        copy.start()
        return copy

    loads = [fetch(src, dst, in_s.at[i]) for i, (src, dst) in enumerate((
        (cols_hbm, cols), (count_hbm, count), (tiles_hbm, tiles), (weight_hbm, weight),
        (bias_hbm, bias), (grad_hbm, grad_hidden)))]
    x_mine = [fetch(feats.at[:, pl.ds(rows_of(r, core), tr)],
                    x_pair.at[r, pl.ds(0, fd)], xa_s.at[r]) for r in range(zs)]
    x_other = [fetch(feats.at[:, pl.ds(rows_of(r, 1 - core), tr)],
                     x_send.at[r], xb_s.at[r]) for r in range(zs)]
    for i in range(4):
        loads[i].wait()
    w_pair[0:fd, :] = weight[...]

    degree = jnp.zeros((tr, 1), F32)
    live = count[0, 0]

    def listed(block):
        where = jnp.int32(0)
        alive = jnp.int32(0)
        for s in range(slots):
            hit = cols[0, 0, s] == block
            where = jnp.where(hit, s, where)
            alive = jnp.where(hit, jnp.where(s < live, 1, 0), alive)
        return tiles[where].astype(F32) * alive.astype(F32)

    for r in range(zs):
        other = listed(zrel[r] * 2 + 1 - core)
        a_send[:, r * tr:(r + 1) * tr] = other.astype(BF16)
        mine = listed(zrel[r] * 2 + core)
        a_pair[0:tr, r * tr:(r + 1) * tr] = mine.astype(BF16)
        degree = degree + jnp.sum(mine + other, axis=1, keepdims=True)
    pl.semaphore_wait(barrier, len(peers))
    ex_w = push(weight_hbm, w_pair.at[pl.ds(fd, fd)], ex_s.at[1], ex_r.at[1], mate)
    ex_x = {r: push(feats.at[:, pl.ds(rows_of(r, 1 - core), tr)],
                    x_pair.at[r, pl.ds(fd, fd)], xs_s.at[r], xs_r.at[r], mate)
            for r in far + [0]}
    ex_a = push(a_send, a_pair.at[pl.ds(tr, tr)], ex_s.at[2], ex_r.at[2], mate)
    row_scale = lax.rsqrt(degree)
    for i in range(4, 6):
        loads[i].wait()
    for copy in x_mine + x_other:
        copy.wait()
    ex_w.wait_recv()

    def hs(k):
        return slice(k * hc, (k + 1) * hc)

    ks = range(CHUNKS)

    def send_terms(k, make, out, into, ss, rr):
        copies = []
        for r in far:
            out[k, r] = make(k, r).astype(BF16)
            copies.append(push(out.at[k, r], into.at[k, r], ss.at[k, r], rr.at[k, r], z_peer(r)))
        return make(k, 0), copies

    def take_terms(k, kept, copies, into):
        for copy in copies:
            copy.wait_recv()
        for r in far:
            kept = kept + into[k, r].astype(F32)
        return kept.astype(BF16)

    def gather_send(k, buf, ss, rr):
        return {r: push(buf.at[k, 0], buf.at[k, r], ss.at[k, r], rr.at[k, r], z_peer(r))
                for r in far}

    def project(k, r):
        if k == 0:
            ex_x[r].wait_recv()
        return tn(x_pair[r], w_pair[:, hs(k)])

    state = [send_terms(k, project, rs_out, rs_in, rs_s, rs_r) for k in ks]
    waits = []
    for k in ks:
        gath[k, 0] = take_terms(k, *state[k], rs_in)
        waits.append(gather_send(k, gath, ag_s, ag_r))
    ex_a.wait_recv()
    mine_sum, parts = [], []
    for k in ks:
        for r in far:
            waits[k][r].wait_recv()
        both = nn(a_pair[...], gath[k].reshape(zs * tr, hc))
        part_out[k] = both[tr:]
        parts.append(push(part_out.at[k], part_in.at[k], p_s.at[k], p_r.at[k], mate))
        mine_sum.append(both[:tr])
    scs = []
    for k in ks:
        parts[k].wait_recv()
        v = (mine_sum[k] + part_in[k]) * row_scale + bias[:, hs(k)]
        v2 = v * v
        t = jnp.tanh(ROOT * (v + 0.044715 * v2 * v))
        hidden[:, hs(k)] = (0.5 * v * (1.0 + t)).astype(BF16)
        slope = 0.5 * (1.0 + t) + 0.5 * v * (1.0 - t * t) * (ROOT * (1.0 + 3 * 0.044715 * v2))
        grad_pre = grad_hidden[:, hs(k)].astype(F32) * slope
        sc_pair[k, 0:tr] = (grad_pre * row_scale).astype(BF16)
        scs.append(push(sc_pair.at[k, pl.ds(0, tr)], sc_pair.at[k, pl.ds(tr, tr)],
                        s_s.at[k], s_r.at[k], mate))

    def terms(k, r):
        if r == zs - 1:
            scs[k].wait_recv()
        return tn(a_pair[:, r * tr:(r + 1) * tr], sc_pair[k])

    state = [send_terms(k, terms, rt_out, rt_in, rt_s, rt_r) for k in ks]
    waits = []
    fwd = [dict() for _ in ks]

    def forward(k, r):
        fwd[k][r] = push(ggath.at[k, r], gfwd.at[k, r], fw_s.at[k, r], fw_r.at[k, r], mate)

    for k in ks:
        ggath[k, 0] = take_terms(k, *state[k], rt_in)
        waits.append(gather_send(k, ggath, gg_s, gg_r))
        forward(k, 0)
    node_state = []
    scale = 1.0 / math.sqrt(total)

    for k in ks:
        for r in range(1, zs):
            waits[k][r].wait_recv()
            forward(k, r)
        acc = jnp.zeros((fd, hc), F32)
        for r in range(zs):
            acc = acc + nn(x_pair[r, 0:fd, :], ggath[k, r])
        for r in range(zs):
            fwd[k][r].wait_recv()
            acc = acc + nn(x_send[r], gfwd[k, r])
        wg_in[k, 0] = acc.astype(BF16)
        node_state.append([push(wg_in.at[k, 0], wg_in.at[k, n], wg_s.at[k, n], wg_r.at[k, n],
                                n_peer(n)) for n in reversed(range(1, nodes))])
    for r in range(zs):
        for parity, buf in ((core, ggath), (1 - core, gfwd)):
            total_rows = nt(weight[:, hs(0)], buf[0, r])
            for k in range(1, CHUNKS):
                total_rows = total_rows + nt(weight[:, hs(k)], buf[k, r])
            grad_feat[:, pl.ds(rows_of(r, parity), tr)] = total_rows.astype(BF16)
    for k in ks:
        for copy in node_state[k]:
            copy.wait_recv()
        level = [wg_in[k, n].astype(F32) for n in range(nodes)]
        while len(level) > 1:
            level = [level[i] + level[i + 1] for i in range(0, len(level), 2)]
        weight_grad[:, hs(k)] = level[0] * scale
    for copy in sent:
        copy.wait_send()


def write_out(a, b, c, a_out, b_out, c_out, sems):
    pairs = ((a, a_out), (b, b_out), (c, c_out))
    copies = [pltpu.make_async_copy(x, y, sems.at[i]) for i, (x, y) in enumerate(pairs)]
    for copy in copies:
        copy.start()
    for copy in copies:
        copy.wait()


def body(node_features, weight, out_bias, edge_tiles, tile_column, tile_count, grad_hidden):
    fd, _, rows = node_features.shape
    blocks = lax.axis_size("feat")
    nodes = lax.axis_size("node")
    zs = blocks // 2
    tr = rows // blocks
    hw = weight.shape[1]
    hc = hw // CHUNKS
    slots = edge_tiles.shape[2]
    sizes = (zs, nodes, slots, tr, fd, hw, nodes * rows)
    vmem = pl.BlockSpec(memory_space=pltpu.VMEM)
    hbm = pl.BlockSpec(memory_space=pltpu.HBM)
    dma = pltpu.SemaphoreType.DMA
    c = CHUNKS
    scratch = [
        pltpu.SMEM((1, 1, slots), jnp.int32),
        pltpu.SMEM((1, 1), jnp.int32),
        pltpu.VMEM((fd, hw), BF16),
        pltpu.VMEM((1, hw), F32),
        pltpu.VMEM((slots, tr, tr), BF16),
        pltpu.VMEM((tr, hw), BF16),
        dma((6,)),
        dma((zs,)),
        dma((zs,)),
        dma((zs,)),
        dma((zs,)),
        pltpu.VMEM((zs, fd, tr), BF16),
        pltpu.VMEM((zs, 2 * fd, tr), BF16),
        pltpu.VMEM((2 * fd, hw), BF16),
        pltpu.VMEM((tr, zs * tr), BF16),
        pltpu.VMEM((2 * tr, zs * tr), BF16),
        pltpu.VMEM((c, zs, tr, hc), BF16),
        pltpu.VMEM((c, zs, tr, hc), BF16),
        pltpu.VMEM((c, zs, tr, hc), BF16),
        pltpu.VMEM((c, tr, hc), F32),
        pltpu.VMEM((c, tr, hc), F32),
        pltpu.VMEM((c, 2 * tr, hc), BF16),
        pltpu.VMEM((c, zs, tr, hc), BF16),
        pltpu.VMEM((c, zs, tr, hc), BF16),
        pltpu.VMEM((c, zs, tr, hc), BF16),
        pltpu.VMEM((c, zs, tr, hc), BF16),
        pltpu.VMEM((c, nodes, fd, hc), BF16),
    ]
    for shape in ((3,), (c, zs), (c, zs), (c,), (c,), (c, zs), (c, zs), (c, zs), (c, nodes)):
        scratch += [dma(shape), dma(shape)]
    hidden, grad_feat, weight_grad = pl.pallas_call(
        functools.partial(kernel, sizes),
        out_shape=(
            jax.ShapeDtypeStruct((tr, hw), BF16),
            jax.ShapeDtypeStruct((fd, rows), BF16),
            jax.ShapeDtypeStruct((fd, hw), F32),
        ),
        in_specs=[hbm] * 7,
        out_specs=(vmem, vmem, vmem),
        scratch_shapes=scratch,
        compiler_params=pltpu.CompilerParams(
            collective_id=0, has_side_effects=True, vmem_limit_bytes=63 * 1024 * 1024
        ),
        name="sage",
    )(
        tile_column,
        tile_count,
        node_features.reshape(fd, rows),
        weight,
        out_bias.reshape(1, hw),
        edge_tiles.reshape(slots, tr, tr),
        grad_hidden.reshape(tr, hw),
    )
    hidden, grad_feat, weight_grad = pl.pallas_call(
        write_out,
        out_shape=(
            jax.ShapeDtypeStruct((tr, hw), BF16),
            jax.ShapeDtypeStruct((fd, rows), BF16),
            jax.ShapeDtypeStruct((fd, hw), F32),
        ),
        in_specs=[vmem] * 3,
        out_specs=(hbm,) * 3,
        scratch_shapes=[dma((3,))],
        name="write_out",
    )(hidden, grad_feat, weight_grad)
    return (hidden[None], grad_feat[:, None, :], weight_grad)


def solution(mesh):
    return jax.shard_map(
        body,
        mesh=mesh,
        in_specs=(
            P("feat", "node", None),
            P("feat", None),
            P(),
            P("node", "feat", None, None, None),
            P("node", "feat", None),
            P("node", "feat"),
            P("node", "feat", None),
        ),
        out_specs=(P("node", "feat", None), P("feat", "node", None), P("feat", None)),
        check_vma=False,
    )
```

time: 54.7 us -> 43.9 us (0.80)
  local copies, waits for them, and re-layouts: 6.23 us -> 0 us
  Pallas kernels: 46.8 us -> 42.4 us
    unnamed x15 -> x0, local copies, waits for them, and re-layouts: 6.23 us -> none
    pallas_call x1, Pallas kernels: 46.8 us -> 40.6 us  [body(): pl.pallas_call(functools.partial(kernel, sizes), out_shape=(jax.ShapeDtyp...]
    pallas_call x0 -> x1, Pallas kernels: none -> 1.8 us  [body(): pl.pallas_call(write_out, out_shape=(jax.ShapeDtypeStruct((tr, hw), BF16)...]
where the time goes in v2:
time: 43.9 us; the launch traced here: 43.7 us
  Pallas kernels  42.4 us (97%)
  between operations  1.29 us (3%)
    pallas_call x1, Pallas kernels, body(): pl.pallas_call(functools.partial(kernel, sizes), out_shape=(jax.ShapeDtyp...  40.6 us
    pallas_call x1, Pallas kernels, body(): pl.pallas_call(write_out, out_shape=(jax.ShapeDtypeStruct((tr, hw), BF16)...  1.8 us

profile of v2, /device:TPU:0, one launch (start us, length us, event | category | flops | bytes accessed | tf_op | source)
XLA Modules:
  0.0 43.7 jit_solution(4019990764510734988)
XLA Ops:
  1.3 40.6 %sage.1 = (bf16[128,256]{1,0:T(8,128)(2,1)}, bf16[128,1024]{1,0:T(8,128)(2,1)}, f32[128,256]{1,0:T(8,128)}) custom-call(s32[1,1,8]{2,1,0:T(1,128)} %cols_hbm.1, s32[1,1]{1,0:T(1,128)S(6)} %copy.10.count_hbm, bf16[128,1024]{1,0:T(8,128)(2,1)} %bitcast.6, bf16[128,256]{1,0:T(8,128)(2,1)} %weight_hbm.1, f32[1,256]{1,0:T(1,128)} %bitcast.9, ...), custom_call_target="tpu_custom_call" | custom-call | tf_op jit(solution)/shard_map/sage/pallas_call | solution.py:289
  41.9 1.8 %write_out.1 = (bf16[128,256]{1,0:T(8,128)(2,1)}, bf16[128,1024]{1,0:T(8,128)(2,1)}, f32[128,256]{1,0:T(8,128)}) custom-call(bf16[128,256]{1,0:T(8,128)(2,1)} %get-tuple-element.9.a, bf16[128,1024]{1,0:T(8,128)(2,1)} %get-tuple-element.10.b, f32[128,256]{1,0:T(8,128)} %get-tuple-element.11.c), custom_call_target="tpu_custom_call" | custom-call | tf_op jit(solution)/shard_map/write_out/pallas_call | solution.py:312
